TPU v7x, 128 devices: a whole 4x4x4 slice. The times are simulated.
128 devices in a mesh: lat: 16 (over x, y), var: 8 (over z, core).
Axes of the slice: x: 4, y: 4, z: 4, core: 2. Of those that a mesh axis runs over, the one named last changes fastest.
Arguments:
- patches: bfloat16 [96, 192, 1024], P('lat', 'var'), may hold values from -6 to 6
- norm_gain: float32 [1024], replicated, may hold values from 0.25 to 1.75
- input_proj: bfloat16 [1024, 3072], replicated, may hold values from -7 to 7
- output_proj: bfloat16 [1024, 1024], replicated, may hold values from -0.1875 to 0.1875
- level_scale: float32 [40, 1024], P('var'), may hold values from 0.1 to 1.9
- level_shift: float32 [40, 1024], P('var'), may hold values from -3 to 3
- head_weight: bfloat16 [40, 1024, 320], P('var', 'lat'), may hold values from -0.1875 to 0.1875
- targets: bfloat16 [40, 96, 192, 320], P('var', 'lat'), may hold values from -6 to 6
- level_counts: int32 [4], replicated, may hold values from 13 to 37
- tile_dataset: int32 [16, 8], P('lat'), may hold values from 0 to 3
- slot_level: int32 [40], P('var'), may hold values from 0 to 39, as said below
Outputs:
- latent: bfloat16 [96, 192, 1024], P('lat', 'var')
- grad_latent: bfloat16 [96, 192, 1024], P('lat', 'var')
- grad_head: float32 [40, 1024, 320], P('var', 'lat')
Inputs may be any that keep to these rules, and one draw needn't show every extreme that they name: `slot_level`: for each j, slots j * 5 to (j + 1) * 5 - 1 hold the levels j * 5 to (j + 1) * 5 - 1 in some order.
All inputs are finite; a program needn't handle non-finite values.
Results may differ from a plain program's by a relative error of at most 0.012.
Values may be sent and summed in bfloat16 or wider, within the bound.
A program may use at most 128 MiB of HBM per device.

v0:
```python
import math
import jax
import jax.numpy as jnp
from jax import lax
from jax.sharding import PartitionSpec as P

HEADS = 16
WH = 6
WW = 12
EPS = 1e-05


def padded(array, sides, width, wrap):
    for axis, dim in sides:
        size, length = (lax.axis_size(axis), array.shape[dim])
        up = [(i, (i + 1) % size) for i in range(size if wrap else size - 1)]
        down = [(j, i) for i, j in up]
        last = lax.slice_in_dim(array, length - width, length, axis=dim)
        initial = lax.slice_in_dim(array, 0, width, axis=dim)
        before = lax.ppermute(last, axis, up)
        after = lax.ppermute(initial, axis, down)
        array = jnp.concatenate([before, array, after], axis=dim)
    return array


def layer_norm(values, gain):
    wide = values.astype(jnp.float32)
    average = jnp.mean(wide, axis=-1, keepdims=True)
    centred = wide - average
    variance = jnp.mean(centred * centred, axis=-1, keepdims=True)
    return (centred * lax.rsqrt(variance + EPS) * gain).astype(jnp.bfloat16)


def window_attention(query_ext, keyval, row_valid, heads):
    ext_rows, ext_cols, width = query_ext.shape
    head_size = width // heads
    win_rows = ext_rows // WH
    win_cols = ext_cols // WW

    def split(values, parts):
        shaped = values.reshape(win_rows, WH, win_cols, WW, parts, heads, head_size)
        return shaped.transpose(0, 2, 1, 3, 4, 5, 6).reshape(
            win_rows * win_cols, WH * WW, parts, heads, head_size
        )

    query_win = split(query_ext, 1)[:, :, 0]
    pairs = split(keyval, 2)
    key_win = pairs[:, :, 0]
    value_win = pairs[:, :, 1]
    key_mask = jnp.broadcast_to(
        row_valid.reshape(win_rows, 1, WH, 1), (win_rows, win_cols, WH, WW)
    ).reshape(win_rows * win_cols, WH * WW)
    scores = jnp.einsum(
        "wqhd,wkhd->whqk", query_win, key_win, preferred_element_type=jnp.float32
    ) / math.sqrt(head_size)
    scores = jnp.where(key_mask[:, None, None, :], scores, -jnp.inf)
    peak = jnp.max(scores, axis=-1, keepdims=True)
    weights = jnp.exp(scores - peak)
    probs = (weights / jnp.sum(weights, axis=-1, keepdims=True)).astype(jnp.bfloat16)
    mixed = jnp.einsum("whqk,wkhd->wqhd", probs, value_win, preferred_element_type=jnp.float32)
    return (
        mixed.reshape(win_rows, win_cols, WH, WW, width)
        .transpose(0, 2, 1, 3, 4)
        .reshape(ext_rows, ext_cols, width)
    )


def slot_terms(piece, target_rows, live_cols, level_scale, level_shift, heads_full):
    piece_wide = piece.astype(jnp.float32)
    rows = (
        piece_wide[None] * level_scale[:, None, None, :] + level_shift[:, None, None, :]
    ).astype(jnp.bfloat16)
    predicted = jnp.einsum("krnd,kdo->krno", rows, heads_full, preferred_element_type=jnp.float32)
    errors = ((predicted - target_rows.astype(jnp.float32)) * live_cols[:, None, :, None]).astype(
        jnp.bfloat16
    )
    back_grad = jnp.einsum("krno,kdo->krnd", errors, heads_full, preferred_element_type=jnp.float32)
    piece_grad = jnp.sum(back_grad * level_scale[:, None, None, :], axis=0)
    head_add = jnp.einsum("krnd,krno->dko", rows, errors, preferred_element_type=jnp.float32)
    return (piece_grad, head_add)


def local(
    patches,
    norm_gain,
    input_proj,
    output_proj,
    level_scale,
    level_shift,
    head_weight,
    targets,
    level_counts,
    tile_dataset,
    slot_level,
):
    band_rows, band_cols, width = patches.shape
    half_rows = WH // 2
    half_cols = WW // 2
    lat_count = lax.axis_size("lat")
    var_count = lax.axis_size("var")
    lat_place = lax.axis_index("lat")
    ext_rows = band_rows + WH
    ext_cols = band_cols + WW
    extended = padded(patches, (("lat", 0),), half_rows, False)
    extended = padded(extended, (("var", 1),), half_cols, True)
    normed_ext = layer_norm(extended, norm_gain)
    keyval = jnp.dot(
        normed_ext.reshape(-1, width), input_proj[:, width:], preferred_element_type=jnp.float32
    )
    keyval = keyval.astype(jnp.bfloat16).reshape(ext_rows, ext_cols, 2 * width)
    normed = normed_ext[half_rows : half_rows + band_rows, half_cols : half_cols + band_cols]
    queries = jnp.dot(
        normed.reshape(-1, width), input_proj[:, :width], preferred_element_type=jnp.float32
    )
    queries = queries.astype(jnp.bfloat16).reshape(band_rows, band_cols, width)
    query_ext = jnp.pad(queries, ((half_rows, WH - half_rows), (half_cols, WW - half_cols), (0, 0)))
    global_row = lat_place * band_rows - half_rows + jnp.arange(ext_rows, dtype=jnp.int32)
    row_valid = (global_row >= 0) & (global_row < lat_count * band_rows)
    mixed = window_attention(query_ext, keyval, row_valid, HEADS)
    attn = mixed[half_rows : half_rows + band_rows, half_cols : half_cols + band_cols].astype(
        jnp.bfloat16
    )
    update = jnp.dot(
        attn.reshape(-1, width), output_proj, preferred_element_type=jnp.float32
    ).reshape(band_rows, band_cols, width)
    latent = (patches.astype(jnp.float32) + update).astype(jnp.bfloat16)
    dataset_row = tile_dataset[0]
    dataset_ids = jnp.arange(level_counts.shape[0], dtype=jnp.int32)
    tile_levels = jnp.sum(
        jnp.where(dataset_row[:, None] == dataset_ids[None, :], level_counts[None, :], 0), axis=1
    )
    live_tiles = (slot_level[None, :] < tile_levels[:, None]).astype(jnp.float32)
    heads_full = lax.all_gather(head_weight, "lat", axis=1, tiled=True)
    tile_ids = jnp.arange(var_count, dtype=jnp.int32)
    piece = lax.all_gather(latent, "var", axis=1, tiled=True)
    piece_cols = piece.shape[1]
    column_tile = jnp.arange(piece_cols, dtype=jnp.int32) // band_cols
    onehot = (column_tile[:, None] == tile_ids[None, :]).astype(jnp.float32)
    column_live = jnp.dot(onehot, live_tiles)
    piece_grad, head_add = slot_terms(
        piece, targets, column_live.T, level_scale, level_shift, heads_full
    )
    latent_terms = piece_grad
    latent_terms, head_terms = (latent_terms, head_add)
    grad_latent = lax.psum_scatter(
        latent_terms.astype(jnp.bfloat16), "var", scatter_dimension=1, tiled=True
    )
    head_terms = head_terms * (1.0 / math.sqrt(lat_count * band_rows * var_count * band_cols))
    share_rows = width // lat_count
    summed = lax.psum(head_terms.astype(jnp.bfloat16), "lat").astype(jnp.float32)
    mine = lax.dynamic_slice_in_dim(summed, lat_place * share_rows, share_rows, 0)
    grad_head = jnp.transpose(mine, (1, 0, 2))
    return (latent, grad_latent, grad_head)


def solution(mesh):
    in_specs = (
        P("lat", "var", None),
        P(),
        P(),
        P(),
        P("var", None),
        P("var", None),
        P("var", "lat", None),
        P("var", "lat", None, None),
        P(),
        P("lat", None),
        P("var"),
    )
    out_specs = (P("lat", "var", None), P("lat", "var", None), P("var", "lat", None))
    return jax.shard_map(local, mesh=mesh, in_specs=in_specs, out_specs=out_specs, check_vma=False)
```

profile of v0, /device:TPU:0, one launch (start us, length us, event | category | flops | bytes accessed | tf_op | source)
XLA Modules:
  0.0 327.8 jit_solution(17000856274102400193)
XLA Ops:
  8.4 3.6 %collective-permute-start = (bf16[3,24,1024]{2,1,0:T(8,128)(2,1)S(1)}, bf16[3,24,1024]{2,1,0:T(8,128)(2,1)S(1)}, u32[]{:S(2)}, u32[]{:S(2)}) collective-permute-start(bf16[3,24,1024]{2,1,0:T(8,128)(2,1)S(1)} %get-tuple-element.25), channel_id=1, source_target_pairs={{0,8},{8,16},{16,24},{24,32},{32,40},{40,48},{48,56},{56,64},{64,7... | collective-permute-start | bytes 442376 | tf_op jit(solution)/shard_map/ppermute | solution.py:20
  13.3 1.8 collective-permute-done
  16.0 3.1 collective-permute-done.1
  19.3 2.9 collective-permute-start.3
  22.4 3.2 collective-permute-done.2
  26.1 1.9 multiply_reduce_fusion.1
  29.8 2.6 reshape.102
  33.7 2.1 fusion.40
  35.9 2.1 reshape.99
  38.0 3.2 copy.47
  41.2 5.5 %fusion.15 = bf16[432,2048]{1,0:T(8,128)(2,1)} fusion(bf16[1024,3072]{1,0:T(8,128)(2,1)} %param.13, f32[432,1024]{1,0:T(8,128)S(1)} %copy-done.3, f32[1024]{0:T(1024)S(1)} %copy-done.5, f32[432]{0:T(512)S(1)} %rsqrt.13, f32[432]{0:T(512)S(1)} %div.33), kind=kOutput, calls=%fused_computation.22 | convolution fusion | flops 1814593536 | bytes 7740800 | tf_op jit(solution)/shard_map/dot_general | solution.py:107
  46.8 6.4 %reshape_reshape.3 = bf16[2,6,3,12,2,16,64]{6,5,4,3,2,1,0:T(8,128)(2,1)} reshape(bf16[432,2048]{1,0:T(8,128)(2,1)} %fusion.15) | data formatting | bytes 3538944 | tf_op jit(solution)/shard_map/reshape;reshape | solution.py:41
  53.1 2.6 copy.45
  55.8 2.7 fusion.59
  58.4 4.0 %copy.59 = bf16[6,72,1,16,64]{1,4,3,0,2:T(8,128)(2,1)} copy(bf16[6,72,1,16,64]{4,3,2,1,0:T(8,128)(2,1)} %get-tuple-element.18) | data formatting | bytes 1769472
  62.5 4.0 %copy.60 = bf16[6,72,1,16,64]{1,4,3,0,2:T(8,128)(2,1)} copy(bf16[6,72,1,16,64]{4,3,2,1,0:T(8,128)(2,1)} %get-tuple-element.19) | data formatting | bytes 1769472
  66.5 3.1 fusion.25
  69.6 1.8 fusion.62
  71.4 1.9 fusion.34
  73.3 4.0 %copy.51 = bf16[6,72,16,64]{3,2,1,0:T(8,128)(2,1)} copy(bf16[6,72,16,64]{1,3,2,0:T(8,128)(2,1)} %fusion.34) | data formatting | bytes 1769472 | tf_op jit(solution)/shard_map/whqk,wkhd->wqhd/transpose | solution.py:60
  77.3 3.9 %reshape.100 = bf16[2,3,6,12,1024]{4,3,2,1,0:T(8,128)(2,1)} reshape(bf16[6,72,16,64]{3,2,1,0:T(8,128)(2,1)} %copy.51) | data formatting | bytes 1769472 | tf_op jit(solution)/shard_map/reshape | solution.py:62
  83.7 2.3 fusion.43
  87.1 28.4 %all-gather.3.cloned.1.call-done = bf16[6,192,1024]{2,1,0:T(8,128)(2,1)} async-done(((bf16[6,24,1024]{2,1,0:T(8,128)(2,1)}), bf16[6,192,1024]{2,1,0:T(8,128)(2,1)}) %all-gather.3.cloned.1.call-update) | async-done | bytes 2359312 | tf_op jit(solution)/shard_map/all_gather | solution.py:135
  115.6 4.4 %convert_element_type.69 = f32[6,192,1024]{2,1,0:T(8,128)} convert(bf16[6,192,1024]{2,1,0:T(8,128)(2,1)} %all-gather.3.cloned.1.call-done) | non-fusion elementwise | flops 1179648 | bytes 7077888 | tf_op jit(solution)/shard_map/convert_element_type | solution.py:69
  119.9 48.6 %all-gather.5.cloned.1.call-done = bf16[5,1024,320]{2,1,0:T(8,128)(2,1)} async-done(((bf16[5,64,320]{2,1,0:T(8,128)(2,1)}), bf16[5,1024,320]{2,1,0:T(8,128)(2,1)}) %all-gather.5.cloned.1.call-update) | async-done | bytes 3276816 | tf_op jit(solution)/shard_map/all_gather | solution.py:133
  168.5 10.1 %multiply_convert_fusion = bf16[5,6,192,320]{3,2,1,0:T(8,128)(2,1)S(1)} fusion(bf16[5,6,192,320]{3,2,1,0:T(8,128)(2,1)} %param.18, f32[5,192]{1,0:T(8,128)S(1)} %fusion.52, bf16[5,1024,320]{2,1,0:T(8,128)(2,1)} %all-gather.5.cloned.1.call-done, f32[5,1024]{1,0:T(8,128)S(1)} %copy-done.6, f32[5,1024]{1,0:T(8,128)S(1)} %copy-done.7, ...), kind=kOutput, calls=%fused_computation.11 | convolution fusion | flops 3799941120 | bytes 15412992 | tf_op jit(solution)/shard_map/krnd,kdo->krno/dot_general | solution.py:73
  178.6 2.1 copy-done.11
  180.8 6.6 %fusion.14 = bf16[1024,5,320]{0,2,1:T(8,128)(2,1)} fusion(bf16[5,6,192,320]{3,2,1,0:T(8,128)(2,1)S(1)} %multiply_convert_fusion, f32[5,1024]{1,0:T(8,128)S(1)} %copy-done.6, f32[5,1024]{1,0:T(8,128)S(1)} %copy-done.7, f32[6,192,1024]{2,1,0:T(8,128)S(1)} %copy-done.2), kind=kOutput, calls=%fused_computation.21 | convolution fusion | flops 3795845120 | bytes 11722752 | tf_op jit(solution)/shard_map/krnd,krno->dko/dot_general | solution.py:79
  187.5 9.9 %multiply_reduce_fusion = bf16[6,192,1024]{2,1,0:T(8,128)(2,1)S(1)} fusion(f32[5,1024]{1,0:T(8,128)S(1)} %copy-done.7, bf16[5,6,192,320]{3,2,1,0:T(8,128)(2,1)} %copy-done.11, bf16[5,1024,320]{2,1,0:T(8,128)(2,1)} %all-gather.5.cloned.1.call-done), kind=kOutput, calls=%fused_computation.1 | convolution fusion | flops 3785490432 | bytes 9342976 | tf_op jit(solution)/shard_map/krno,kdo->krnd/dot_general | solution.py:77
  197.4 1.7 copy.61
  199.1 84.3 %all-reduce.3.cloned.1.call-done = bf16[1024,5,320]{0,2,1:T(8,128)(2,1)} async-done(((bf16[1024,5,320]{0,2,1:T(8,128)(2,1)}), bf16[1024,5,320]{0,2,1:T(8,128)(2,1)}) %all-reduce.3.cloned.1.call-update) | async-done | bytes 3276816 | tf_op jit(solution)/shard_map/psum | solution.py:150
  285.6 33.4 %reduce-scatter.4.cloned.1.call-done = bf16[24,6144]{1,0:T(8,128)(2,1)} async-done(((bf16[192,6144]{1,0:T(8,128)(2,1)}), bf16[24,6144]{1,0:T(8,128)(2,1)}) %reduce-scatter.4.cloned.1.call-update) | async-done | bytes 294928
  (60 shorter events, 15.7 us)
Async XLA Ops:
  7.2 76.5 %copy-start = (bf16[1024,1024]{1,0:T(8,128)(2,1)S(1)}, bf16[1024,1024]{1,0:T(8,128)(2,1)}, u32[]{:S(2)}) copy-start(bf16[1024,1024]{1,0:T(8,128)(2,1)} %param.14) | copy-start | bytes 6291460
  7.2 108.4 %all-gather.3.cloned.1.call-start = ((), (), s32[]{:S(2)}) async-start(), calls=%async_computation.1 | async-start | bytes 2654208 | tf_op jit(solution)/shard_map/all_gather | solution.py:135
  8.4 6.7 %collective-permute-start = (bf16[3,24,1024]{2,1,0:T(8,128)(2,1)S(1)}, bf16[3,24,1024]{2,1,0:T(8,128)(2,1)S(1)}, u32[]{:S(2)}, u32[]{:S(2)}) collective-permute-start(bf16[3,24,1024]{2,1,0:T(8,128)(2,1)S(1)} %get-tuple-element.25), channel_id=1, source_target_pairs={{0,8},{8,16},{16,24},{24,32},{32,40},{40,48},{48,56},{56,64},{64,7... | collective-permute-start | bytes 442376 | tf_op jit(solution)/shard_map/ppermute | solution.py:20
  12.0 7.2 %collective-permute-start.1 = (bf16[3,24,1024]{2,1,0:T(8,128)(2,1)S(1)}, bf16[3,24,1024]{2,1,0:T(8,128)(2,1)S(1)}, u32[]{:S(2)}, u32[]{:S(2)}) collective-permute-start(bf16[3,24,1024]{2,1,0:T(8,128)(2,1)S(1)} %get-tuple-element.24), channel_id=1, source_target_pairs={{8,0},{16,8},{24,16},{32,24},{40,32},{48,40},{56,48},{64,56},{72,6... | collective-permute-start | bytes 442376 | tf_op jit(solution)/shard_map/ppermute | solution.py:21
  19.2 6.3 %collective-permute-start.2 = (bf16[12,6,1024]{2,1,0:T(8,128)(2,1)S(1)}, bf16[12,6,1024]{2,1,0:T(8,128)(2,1)S(1)}, u32[]{:S(2)}, u32[]{:S(2)}) collective-permute-start(bf16[12,6,1024]{2,1,0:T(8,128)(2,1)S(1)} %get-tuple-element.22), channel_id=1, source_target_pairs={{0,1},{1,2},{2,3},{3,4},{4,5},{5,6},{6,7},{7,0},{8,9},{9,10},{10,1... | collective-permute-start | bytes 442376 | tf_op jit(solution)/shard_map/ppermute | solution.py:20
  19.3 6.3 %collective-permute-start.3 = (bf16[12,6,1024]{2,1,0:T(8,128)(2,1)S(1)}, bf16[12,6,1024]{2,1,0:T(8,128)(2,1)S(1)}, u32[]{:S(2)}, u32[]{:S(2)}) collective-permute-start(bf16[12,6,1024]{2,1,0:T(8,128)(2,1)S(1)} %get-tuple-element.23), channel_id=1, source_target_pairs={{1,0},{2,1},{3,2},{4,3},{5,4},{6,5},{7,6},{0,7},{9,8},{10,9},{11,1... | collective-permute-start | bytes 442376 | tf_op jit(solution)/shard_map/ppermute | solution.py:21
  27.9 4.4 %copy-start.5 = (f32[1024]{0:T(1024)S(1)}, f32[1024]{0:T(1024)}, u32[]{:S(2)}) copy-start(f32[1024]{0:T(1024)} %param.12) | copy-start | bytes 12292
  38.0 3.2 copy-start.3
  69.6 1.8 copy-start.4
  82.6 4.2 %copy-start.8 = (s32[4]{0:T(128)S(1)}, s32[4]{0:T(128)}, u32[]{:S(2)}) copy-start(s32[4]{0:T(128)} %param.19) | copy-start | bytes 52
  82.6 4.2 %copy-start.9 = (s32[1,8]{1,0:T(1,128)S(1)}, s32[1,8]{1,0:T(1,128)}, u32[]{:S(2)}) copy-start(s32[1,8]{1,0:T(1,128)} %param.20) | copy-start | bytes 100
  82.6 4.3 %copy-start.10 = (s32[5]{0:T(128)S(1)}, s32[5]{0:T(128)}, u32[]{:S(2)}) copy-start(s32[5]{0:T(128)} %param.21) | copy-start | bytes 64
  86.0 82.5 %all-gather.5.cloned.1.call-start = ((), (), s32[]{:S(2)}) async-start(), calls=%async_computation.2 | async-start | bytes 4177920 | tf_op jit(solution)/shard_map/all_gather | solution.py:133
  86.7 196.6 %all-reduce.3.cloned.1.call-start = ((), (), s32[]{:S(2)}) async-start(), calls=%async_computation.3 | async-start | bytes 6553600 | tf_op jit(solution)/shard_map/psum | solution.py:150
  87.1 81.4 %copy-start.6 = (f32[5,1024]{1,0:T(8,128)S(1)}, f32[5,1024]{1,0:T(8,128)}, u32[]{:S(2)}) copy-start(f32[5,1024]{1,0:T(8,128)} %param.16) | copy-start | bytes 61444
  87.1 81.4 %copy-start.7 = (f32[5,1024]{1,0:T(8,128)S(1)}, f32[5,1024]{1,0:T(8,128)}, u32[]{:S(2)}) copy-start(f32[5,1024]{1,0:T(8,128)} %param.15) | copy-start | bytes 61444
  168.5 12.3 %copy-start.2 = (f32[6,192,1024]{2,1,0:T(8,128)S(1)}, f32[6,192,1024]{2,1,0:T(8,128)}, u32[]{:S(2)}) copy-start(f32[6,192,1024]{2,1,0:T(8,128)} %convert_element_type.69) | copy-start | bytes 14155780
  178.6 2.2 copy-start.11
  187.4 131.6 %reduce-scatter.4.cloned.1.call-start = ((), (), s32[]{:S(2)}) async-start(), calls=%async_computation.4 | async-start | bytes 2654208
  197.4 123.9 %copy-start.1 = (bf16[1024,1024]{1,0:T(8,128)(2,1)S(1)}, bf16[1024,1024]{1,0:T(8,128)(2,1)}, u32[]{:S(2)}) copy-start(bf16[1024,1024]{1,0:T(8,128)(2,1)} %param.14) | copy-start | bytes 6291460
Sparse Core Ops, SparseCore 0:
  86.1 29.4 all-gather.2
  117.7 50.7 all-gather.4
  187.6 95.7 all-reduce.2
  285.8 33.2 reduce-scatter.3
where the time goes:
time: 329 us; the launch traced here: 328 us
  waiting for transfers between devices  204 us (62%)
  local copies, waits for them, and re-layouts  48 us (15%)
  matrix products  41.6 us (13%)
  between operations  14 us (4%)
  other arithmetic  12.7 us (4%)
  starting transfers between devices  7.98 us (2%)
    psum x1, waiting for transfers between devices, local(): lax.psum(head_terms.astype(jnp.bfloat16), 'lat').astype(jnp.float32)  84.3 us
    all_gather x1, waiting for transfers between devices, local(): heads_full = lax.all_gather(head_weight, 'lat', axis=1, tiled=True)  48.6 us
    unnamed x5, waiting for transfers between devices  34.2 us
    all_gather x1, waiting for transfers between devices, local(): piece = lax.all_gather(latent, 'var', axis=1, tiled=True)  28.4 us
    unnamed x32, local copies, waits for them, and re-layouts  16.3 us
    dot_general x1, matrix products, slot_terms(): jnp.einsum('krnd,kdo->krno', rows, heads_full, preferred_element_type=jnp...  10.1 us
    dot_general x1, matrix products, slot_terms(): jnp.einsum('krno,kdo->krnd', errors, heads_full, preferred_element_type=j...  9.86 us
    another operation x2, local copies, waits for them, and re-layouts, split(): shaped = values.reshape(win_rows, WH, win_cols, WW, parts, heads, head_size)  8.98 us
  transfers between devices with their start and end apart: 8, of which 7 were waited for; matrix products, arithmetic and copies ran while one was open for 6% of the time, Pallas kernels for 0%

commit v1 on v0

--- a/solution.py
+++ b/solution.py
@@ -8,6 +8,13 @@
 WH = 6
 WW = 12
 EPS = 1e-05
+
+
+def swapped_in(block, axis, along):
+    size = lax.axis_size(axis)
+    tiles = jnp.stack([block for _ in range(size)])
+    tiles = lax.all_to_all(tiles, axis, split_axis=0, concat_axis=0)
+    return jnp.concatenate(tiles, axis=along)
 
 
 def padded(array, sides, width, wrap):
@@ -132,7 +139,7 @@
     live_tiles = (slot_level[None, :] < tile_levels[:, None]).astype(jnp.float32)
     heads_full = lax.all_gather(head_weight, "lat", axis=1, tiled=True)
     tile_ids = jnp.arange(var_count, dtype=jnp.int32)
-    piece = lax.all_gather(latent, "var", axis=1, tiled=True)
+    piece = swapped_in(latent, "var", 1)
     piece_cols = piece.shape[1]
     column_tile = jnp.arange(piece_cols, dtype=jnp.int32) // band_cols
     onehot = (column_tile[:, None] == tile_ids[None, :]).astype(jnp.float32)

time: 329 us -> 289 us (0.88)
  waiting for transfers between devices: 204 us -> 156 us
  starting transfers between devices: 7.98 us -> 13.9 us
    all_gather x1, waiting for transfers between devices: 48.6 us -> 0.01 us  [local(): heads_full = lax.all_gather(head_weight, 'lat', axis=1, tiled=True)]
    all_to_all x0 -> x1, waiting for transfers between devices: none -> 29.5 us  [swapped_in(): tiles = lax.all_to_all(tiles, axis, split_axis=0, concat_axis=0)]
    all_gather x1 -> x0, waiting for transfers between devices: 28.4 us -> none  [local(): piece = lax.all_gather(latent, 'var', axis=1, tiled=True)]
    all_to_all x0 -> x1, starting transfers between devices: none -> 5.73 us  [swapped_in(): tiles = lax.all_to_all(tiles, axis, split_axis=0, concat_axis=0)]
    unnamed x5 -> x4, waiting for transfers between devices: 34.2 us -> 33.6 us
    unnamed x32 -> x34, local copies, waits for them, and re-layouts: 16.3 us -> 16.3 us
  transfers between devices with their start and end apart: 8 -> 8, of which waited for: 7 -> 6; matrix products, arithmetic and copies ran while one was open for 6% -> 28% of each run, Pallas kernels for 0% -> 0%
where the time goes in v1:
time: 289 us; the launch traced here: 288 us
  waiting for transfers between devices  156 us (54%)
  local copies, waits for them, and re-layouts  49.9 us (17%)
  matrix products  41 us (14%)
  between operations  14 us (5%)
  starting transfers between devices  13.9 us (5%)
  other arithmetic  12.7 us (4%)
    psum x1, waiting for transfers between devices, local(): lax.psum(head_terms.astype(jnp.bfloat16), 'lat').astype(jnp.float32)  85 us
    unnamed x4, waiting for transfers between devices  33.6 us
    all_to_all x1, waiting for transfers between devices, swapped_in(): tiles = lax.all_to_all(tiles, axis, split_axis=0, concat_axis=0)  29.5 us
    unnamed x34, local copies, waits for them, and re-layouts  16.3 us
    dot_general x1, matrix products, slot_terms(): jnp.einsum('krnd,kdo->krno', rows, heads_full, preferred_element_type=jnp...  9.92 us
    dot_general x1, matrix products, slot_terms(): jnp.einsum('krno,kdo->krnd', errors, heads_full, preferred_element_type=j...  9.86 us
    another operation x2, local copies, waits for them, and re-layouts, split(): shaped = values.reshape(win_rows, WH, win_cols, WW, parts, heads, head_size)  9.06 us
    dot_general x1, matrix products, slot_terms(): jnp.einsum('krnd,krno->dko', rows, errors, preferred_element_type=jnp.flo...  6.63 us
  transfers between devices with their start and end apart: 8, of which 6 were waited for; matrix products, arithmetic and copies ran while one was open for 28% of the time, Pallas kernels for 0%

profile of v1, /device:TPU:0, one launch (start us, length us, event | category | flops | bytes accessed | tf_op | source)
XLA Modules:
  0.0 287.7 jit_solution(17823371605606555132)
XLA Ops:
  8.4 3.6 %collective-permute-start = (bf16[3,24,1024]{2,1,0:T(8,128)(2,1)S(1)}, bf16[3,24,1024]{2,1,0:T(8,128)(2,1)S(1)}, u32[]{:S(2)}, u32[]{:S(2)}) collective-permute-start(bf16[3,24,1024]{2,1,0:T(8,128)(2,1)S(1)} %get-tuple-element.28), channel_id=1, source_target_pairs={{0,8},{8,16},{16,24},{24,32},{32,40},{40,48},{48,56},{56,64},{64,7... | collective-permute-start | bytes 442376 | tf_op jit(solution)/shard_map/ppermute | solution.py:27
  13.3 1.8 collective-permute-done
  16.0 3.1 %collective-permute-done.1 = bf16[3,24,1024]{2,1,0:T(8,128)(2,1)S(1)} collective-permute-done((bf16[3,24,1024]{2,1,0:T(8,128)(2,1)S(1)}, bf16[3,24,1024]{2,1,0:T(8,128)(2,1)S(1)}, u32[]{:S(2)}, u32[]{:S(2)}) %collective-permute-start.1) | collective-permute-done | bytes 147488 | tf_op jit(solution)/shard_map/ppermute | solution.py:28
  19.3 2.9 %collective-permute-start.3 = (bf16[12,6,1024]{2,1,0:T(8,128)(2,1)S(1)}, bf16[12,6,1024]{2,1,0:T(8,128)(2,1)S(1)}, u32[]{:S(2)}, u32[]{:S(2)}) collective-permute-start(bf16[12,6,1024]{2,1,0:T(8,128)(2,1)S(1)} %get-tuple-element.26), channel_id=1, source_target_pairs={{1,0},{2,1},{3,2},{4,3},{5,4},{6,5},{7,6},{0,7},{9,8},{10,9},{11,1... | collective-permute-start | bytes 442376 | tf_op jit(solution)/shard_map/ppermute | solution.py:28
  22.4 3.1 %collective-permute-done.2 = bf16[12,6,1024]{2,1,0:T(8,128)(2,1)S(1)} collective-permute-done((bf16[12,6,1024]{2,1,0:T(8,128)(2,1)S(1)}, bf16[12,6,1024]{2,1,0:T(8,128)(2,1)S(1)}, u32[]{:S(2)}, u32[]{:S(2)}) %collective-permute-start.2) | collective-permute-done | bytes 147488 | tf_op jit(solution)/shard_map/ppermute | solution.py:27
  26.0 1.9 multiply_reduce_fusion.1
  29.8 2.7 reshape.112
  33.7 2.2 fusion.40
  36.1 2.1 reshape.109
  38.2 3.2 %copy.57 = bf16[2,3,6,12,1,16,64]{6,5,3,2,1,0,4:T(8,128)(2,1)} copy(bf16[2,3,6,12,1,16,64]{6,5,3,1,2,0,4:T(8,128)(2,1)} %bitcast.61) | data formatting | bytes 1769472 | tf_op jit(solution)/shard_map/transpose | solution.py:49
  41.5 5.5 %fusion.15 = bf16[432,2048]{1,0:T(8,128)(2,1)} fusion(bf16[1024,3072]{1,0:T(8,128)(2,1)} %param.13, f32[432,1024]{1,0:T(8,128)S(1)} %copy-done.3, f32[1024]{0:T(1024)S(1)} %copy-done.6, f32[432]{0:T(512)S(1)} %rsqrt.13, f32[432]{0:T(512)S(1)} %div.33), kind=kOutput, calls=%fused_computation.22 | convolution fusion | flops 1814593536 | bytes 7740800 | tf_op jit(solution)/shard_map/dot_general | solution.py:114
  47.0 6.5 %reshape_reshape.3 = bf16[2,6,3,12,2,16,64]{6,5,4,3,2,1,0:T(8,128)(2,1)} reshape(bf16[432,2048]{1,0:T(8,128)(2,1)} %fusion.15) | data formatting | bytes 3538944 | tf_op jit(solution)/shard_map/reshape;reshape | solution.py:48
  53.4 2.6 copy.55
  56.0 2.7 fusion.59
  58.7 4.0 %copy.70 = bf16[6,72,1,16,64]{1,4,3,0,2:T(8,128)(2,1)} copy(bf16[6,72,1,16,64]{4,3,2,1,0:T(8,128)(2,1)} %get-tuple-element.21) | data formatting | bytes 1769472
  62.8 4.1 %copy.71 = bf16[6,72,1,16,64]{1,4,3,0,2:T(8,128)(2,1)} copy(bf16[6,72,1,16,64]{4,3,2,1,0:T(8,128)(2,1)} %get-tuple-element.22) | data formatting | bytes 1769472
  66.8 3.1 %fusion.25 = f32[6,16,72,72]{2,3,1,0:T(8,128)S(1)} fusion(bf16[6,72,16,64]{3,2,1,0:T(8,128)(2,1)} %bitcast.62, bf16[6,72,1,16,64]{1,4,3,0,2:T(8,128)(2,1)} %copy.71), kind=kOutput, calls=%fused_computation.30 | convolution fusion | flops 63700992 | bytes 3760128 | tf_op jit(solution)/shard_map/wqhd,wkhd->whqk/dot_general | solution.py:60
  70.0 1.8 fusion.62
  71.8 1.9 fusion.34
  73.7 4.0 %copy.61 = bf16[6,72,16,64]{3,2,1,0:T(8,128)(2,1)} copy(bf16[6,72,16,64]{1,3,2,0:T(8,128)(2,1)} %fusion.34) | data formatting | bytes 1769472 | tf_op jit(solution)/shard_map/whqk,wkhd->wqhd/transpose | solution.py:67
  77.7 3.9 %reshape.110 = bf16[2,3,6,12,1024]{4,3,2,1,0:T(8,128)(2,1)} reshape(bf16[6,72,16,64]{3,2,1,0:T(8,128)(2,1)} %copy.61) | data formatting | bytes 1769472 | tf_op jit(solution)/shard_map/reshape | solution.py:69
  85.7 1.7 stack.2
  87.4 5.7 %all-to-all-start = ((bf16[8,6,24,1024]{3,2,1,0:T(8,128)(2,1)}), bf16[8,6,24,1024]{3,2,1,0:T(8,128)(2,1)}, u32[]{:S(2)}, u32[]{:S(2)}) async-start(bf16[8,6,24,1024]{3,2,1,0:T(8,128)(2,1)} %stack.2), calls=%async_computation | async-start | bytes 4718592 | tf_op jit(solution)/shard_map/all_to_all | solution.py:16
  93.8 29.5 %all-to-all-done = bf16[8,6,24,1024]{3,2,1,0:T(8,128)(2,1)} async-done(((bf16[8,6,24,1024]{3,2,1,0:T(8,128)(2,1)}), bf16[8,6,24,1024]{3,2,1,0:T(8,128)(2,1)}, u32[]{:S(2)}, u32[]{:S(2)}) %all-to-all-start) | async-done | bytes 2359328 | tf_op jit(solution)/shard_map/all_to_all | solution.py:16
  123.3 4.4 %copy_convert_fusion = f32[8,6,24,1024]{3,2,0,1:T(8,128)} fusion(bf16[8,6,24,1024]{3,2,1,0:T(8,128)(2,1)} %all-to-all-done), kind=kLoop, calls=%fused_computation.24 | loop fusion | flops 1179648 | bytes 7077888 | tf_op jit(solution)/shard_map/convert_element_type | solution.py:76
  127.7 9.9 %multiply_convert_fusion = bf16[5,6,192,320]{3,2,1,0:T(8,128)(2,1)S(1)} fusion(bf16[5,6,192,320]{3,2,1,0:T(8,128)(2,1)} %param.18, f32[5,192]{1,0:T(8,128)S(1)} %fusion.52, bf16[5,1024,320]{2,1,0:T(8,128)(2,1)} %all-gather.2.cloned.1.call-done, f32[5,1024]{1,0:T(8,128)S(1)} %copy-done.7, f32[5,1024]{1,0:T(8,128)S(1)} %copy-done.8, f32[6,192,1024]{2,1,0:T(8,128)} %bitcast.63), kind=kOutput, calls=%fused_computation.11 | convolution fusion | flops 3799941120 | bytes 15412992 | tf_op jit(solution)/shard_map/krnd,kdo->krno/dot_general | solution.py:80
  137.6 2.1 copy-done.12
  139.7 6.6 %fusion.14 = bf16[1024,5,320]{0,2,1:T(8,128)(2,1)} fusion(bf16[5,6,192,320]{3,2,1,0:T(8,128)(2,1)S(1)} %multiply_convert_fusion, f32[5,1024]{1,0:T(8,128)S(1)} %copy-done.7, f32[5,1024]{1,0:T(8,128)S(1)} %copy-done.8, f32[6,192,1024]{2,1,0:T(8,128)S(1)} %bitcast.64), kind=kOutput, calls=%fused_computation.21 | convolution fusion | flops 3795845120 | bytes 11722752 | tf_op jit(solution)/shard_map/krnd,krno->dko/dot_general | solution.py:86
  146.4 9.9 %multiply_reduce_fusion = bf16[6,192,1024]{2,1,0:T(8,128)(2,1)S(1)} fusion(f32[5,1024]{1,0:T(8,128)S(1)} %copy-done.8, bf16[5,6,192,320]{3,2,1,0:T(8,128)(2,1)} %copy-done.12, bf16[5,1024,320]{2,1,0:T(8,128)(2,1)} %all-gather.2.cloned.1.call-done), kind=kOutput, calls=%fused_computation.1 | convolution fusion | flops 3785490432 | bytes 9342976 | tf_op jit(solution)/shard_map/krno,kdo->krnd/dot_general | solution.py:84
  156.3 1.7 copy.72
  158.0 85.0 %all-reduce.3.cloned.1.call-done = bf16[1024,5,320]{0,2,1:T(8,128)(2,1)} async-done(((bf16[1024,5,320]{0,2,1:T(8,128)(2,1)}), bf16[1024,5,320]{0,2,1:T(8,128)(2,1)}) %all-reduce.3.cloned.1.call-update) | async-done | bytes 3276816 | tf_op jit(solution)/shard_map/psum | solution.py:157
  245.3 33.6 %reduce-scatter.4.cloned.1.call-done = bf16[24,6144]{1,0:T(8,128)(2,1)} async-done(((bf16[192,6144]{1,0:T(8,128)(2,1)}), bf16[24,6144]{1,0:T(8,128)(2,1)}) %reduce-scatter.4.cloned.1.call-update) | async-done | bytes 294928
  (62 shorter events, 16.7 us)
Async XLA Ops:
  7.2 76.9 %copy-start = (bf16[1024,1024]{1,0:T(8,128)(2,1)S(1)}, bf16[1024,1024]{1,0:T(8,128)(2,1)}, u32[]{:S(2)}) copy-start(bf16[1024,1024]{1,0:T(8,128)(2,1)} %param.14) | copy-start | bytes 6291460
  7.2 120.5 %all-gather.2.cloned.1.call-start = ((), (), s32[]{:S(2)}) async-start(), calls=%async_computation.2 | async-start | bytes 4177920 | tf_op jit(solution)/shard_map/all_gather | solution.py:140
  8.4 6.7 %collective-permute-start = (bf16[3,24,1024]{2,1,0:T(8,128)(2,1)S(1)}, bf16[3,24,1024]{2,1,0:T(8,128)(2,1)S(1)}, u32[]{:S(2)}, u32[]{:S(2)}) collective-permute-start(bf16[3,24,1024]{2,1,0:T(8,128)(2,1)S(1)} %get-tuple-element.28), channel_id=1, source_target_pairs={{0,8},{8,16},{16,24},{24,32},{32,40},{40,48},{48,56},{56,64},{64,7... | collective-permute-start | bytes 442376 | tf_op jit(solution)/shard_map/ppermute | solution.py:27
  12.0 7.2 %collective-permute-start.1 = (bf16[3,24,1024]{2,1,0:T(8,128)(2,1)S(1)}, bf16[3,24,1024]{2,1,0:T(8,128)(2,1)S(1)}, u32[]{:S(2)}, u32[]{:S(2)}) collective-permute-start(bf16[3,24,1024]{2,1,0:T(8,128)(2,1)S(1)} %get-tuple-element.27), channel_id=1, source_target_pairs={{8,0},{16,8},{24,16},{32,24},{40,32},{48,40},{56,48},{64,56},{72,6... | collective-permute-start | bytes 442376 | tf_op jit(solution)/shard_map/ppermute | solution.py:28
  19.2 6.3 %collective-permute-start.2 = (bf16[12,6,1024]{2,1,0:T(8,128)(2,1)S(1)}, bf16[12,6,1024]{2,1,0:T(8,128)(2,1)S(1)}, u32[]{:S(2)}, u32[]{:S(2)}) collective-permute-start(bf16[12,6,1024]{2,1,0:T(8,128)(2,1)S(1)} %get-tuple-element.25), channel_id=1, source_target_pairs={{0,1},{1,2},{2,3},{3,4},{4,5},{5,6},{6,7},{7,0},{8,9},{9,10},{10,1... | collective-permute-start | bytes 442376 | tf_op jit(solution)/shard_map/ppermute | solution.py:27
  19.3 6.3 %collective-permute-start.3 = (bf16[12,6,1024]{2,1,0:T(8,128)(2,1)S(1)}, bf16[12,6,1024]{2,1,0:T(8,128)(2,1)S(1)}, u32[]{:S(2)}, u32[]{:S(2)}) collective-permute-start(bf16[12,6,1024]{2,1,0:T(8,128)(2,1)S(1)} %get-tuple-element.26), channel_id=1, source_target_pairs={{1,0},{2,1},{3,2},{4,3},{5,4},{6,5},{7,6},{0,7},{9,8},{10,9},{11,1... | collective-permute-start | bytes 442376 | tf_op jit(solution)/shard_map/ppermute | solution.py:28
  27.9 4.5 %copy-start.6 = (f32[1024]{0:T(1024)S(1)}, f32[1024]{0:T(1024)}, u32[]{:S(2)}) copy-start(f32[1024]{0:T(1024)} %param.12) | copy-start | bytes 12292
  38.2 3.2 %copy-start.3 = (f32[432,1024]{1,0:T(8,128)S(1)}, f32[432,1024]{1,0:T(8,128)}, u32[]{:S(2)}) copy-start(f32[432,1024]{1,0:T(8,128)} %reshape.112) | copy-start | bytes 5308420
  70.0 1.8 copy-start.4
  85.7 1.7 copy-start.5
  85.7 7.7 %copy-start.9 = (s32[4]{0:T(128)S(1)}, s32[4]{0:T(128)}, u32[]{:S(2)}) copy-start(s32[4]{0:T(128)} %param.19) | copy-start | bytes 52
  85.7 7.7 %copy-start.10 = (s32[1,8]{1,0:T(1,128)S(1)}, s32[1,8]{1,0:T(1,128)}, u32[]{:S(2)}) copy-start(s32[1,8]{1,0:T(1,128)} %param.20) | copy-start | bytes 100
  85.7 7.8 %copy-start.11 = (s32[5]{0:T(128)S(1)}, s32[5]{0:T(128)}, u32[]{:S(2)}) copy-start(s32[5]{0:T(128)} %param.21) | copy-start | bytes 64
  87.4 35.8 %all-to-all-start = ((bf16[8,6,24,1024]{3,2,1,0:T(8,128)(2,1)}), bf16[8,6,24,1024]{3,2,1,0:T(8,128)(2,1)}, u32[]{:S(2)}, u32[]{:S(2)}) async-start(bf16[8,6,24,1024]{3,2,1,0:T(8,128)(2,1)} %stack.2), calls=%async_computation | async-start | bytes 4718592 | tf_op jit(solution)/shard_map/all_to_all | solution.py:16
  93.2 149.9 %all-reduce.3.cloned.1.call-start = ((), (), s32[]{:S(2)}) async-start(), calls=%async_computation.3 | async-start | bytes 6553600 | tf_op jit(solution)/shard_map/psum | solution.py:157
  93.8 33.9 %copy-start.7 = (f32[5,1024]{1,0:T(8,128)S(1)}, f32[5,1024]{1,0:T(8,128)}, u32[]{:S(2)}) copy-start(f32[5,1024]{1,0:T(8,128)} %param.16) | copy-start | bytes 61444
  93.8 33.9 %copy-start.8 = (f32[5,1024]{1,0:T(8,128)S(1)}, f32[5,1024]{1,0:T(8,128)}, u32[]{:S(2)}) copy-start(f32[5,1024]{1,0:T(8,128)} %param.15) | copy-start | bytes 61444
  127.7 12.1 %copy-start.2 = (f32[8,6,24,1024]{3,2,0,1:T(8,128)S(1)}, f32[8,6,24,1024]{3,2,0,1:T(8,128)}, u32[]{:S(2)}) copy-start(f32[8,6,24,1024]{3,2,0,1:T(8,128)} %copy_convert_fusion) | copy-start | bytes 14155780
  137.6 2.2 copy-start.12
  146.4 132.5 %reduce-scatter.4.cloned.1.call-start = ((), (), s32[]{:S(2)}) async-start(), calls=%async_computation.4 | async-start | bytes 2654208
  156.3 124.8 %copy-start.1 = (bf16[1024,1024]{1,0:T(8,128)(2,1)S(1)}, bf16[1024,1024]{1,0:T(8,128)(2,1)}, u32[]{:S(2)}) copy-start(bf16[1024,1024]{1,0:T(8,128)(2,1)} %param.14) | copy-start | bytes 6291460
Sparse Core Ops, SparseCore 0:
  22.3 52.7 all-gather.1
  146.5 96.4 all-reduce.2
  245.6 33.2 reduce-scatter.3
